TPU v7x, 32 devices: a whole 2x2x4 slice. The times are simulated.
32 devices in a mesh: groups: 2 (over y), qry: 4 (over x, core), ref: 4 (over z).
Axes of the slice: x: 2, y: 2, z: 4, core: 2. Of those that a mesh axis runs over, the one named last changes fastest.
Arguments:
- query_feats: bfloat16 [1024, 9, 3840], P(('groups', 'qry')), parts along dimension 0, may hold values from -6 to 6
- ref_feats: bfloat16 [256, 4, 9, 3840], P(('groups', 'ref'), 'qry'), parts along dimension 0, may hold values from -6 to 6
- pair_table: int32 [8, 4], P('groups'), parts along dimension 0, may hold values from 0 to 1, as said below
- lengths: int32 [4], P('groups'), parts along dimension 0, may hold values from 1 to 96, 128 in all
- query_len: int32 [2], P('groups'), parts along dimension 0, may hold values from 64 to 128
- conv1_weight: float32 [3, 3, 32], replicated, may hold values from -2 to 2
- conv1_bias: float32 [32], replicated, may hold values from -3 to 3
- conv2_weight: bfloat16 [3, 3, 64, 32], replicated, may hold values from -0.375 to 0.375
- conv2_bias: float32 [64], replicated, may hold values from -3 to 3
- conv3_weight: bfloat16 [3, 3, 128, 64], replicated, may hold values from -0.25 to 0.25
- conv3_bias: float32 [128], replicated, may hold values from -3 to 3
- conv4_weight: bfloat16 [128], replicated, may hold values from -0.5 to 0.5
- conv4_bias: float32 [1], replicated, may hold values from -3 to 3
Outputs:
- score_map: float32 [256, 128], P(('groups', 'qry'), 'ref'), parts along dimension 0
- video_scores: float32 [4], P('groups'), parts along dimension 0
There are 2 independent parts, one for each index of `groups`. A program takes and returns all parts, laid end to end along the dimension named above; an argument that names none is the same for every part. Nothing has to cross between parts.
Inputs may be any that keep to these rules, and one draw needn't show every extreme that they name: `pair_table`: in each row, at most 1 of the 1 tiles in the block of one index of ref are 1, and some such block holds exactly 1 in every draw.
All inputs are finite; a program needn't handle non-finite values.
Results may differ from a plain program's by a relative error of at most 0.01.
Values may be sent and summed in bfloat16 or wider, within the bound.
No kernel may reach another device: no remote copies, remote signals or barrier semaphores. Data moves between devices by JAX's collectives and lax.ppermute only.
A program may use at most 128 MiB of HBM per device.

v0:
```python
import math
import jax
import jax.numpy as jnp
from jax import lax
from jax.sharding import PartitionSpec as P

MOST = 1


def padded_2(block, sides, width):
    for axis, dim in sides:
        count = lax.axis_size(axis)
        forward = [(i, i + 1) for i in range(count - 1)]
        backward = [(target, source) for source, target in forward]
        low = lax.ppermute(
            lax.slice_in_dim(block, block.shape[dim] - width, None, axis=dim), axis, forward
        )
        high = lax.ppermute(lax.slice_in_dim(block, 0, width, axis=dim), axis, backward)
        block = jnp.concatenate([low, block, high], axis=dim)
    return block


def slot_table(mask, most):
    width = mask.shape[-1]
    ranking = jnp.cumsum(mask, axis=-1) - 1
    slot_ids = jnp.arange(most, dtype=jnp.int32)
    chosen = (mask[..., None, :] == 1) & (ranking[..., None, :] == slot_ids[:, None])
    picked = jnp.sum(jnp.where(chosen, jnp.arange(width, dtype=jnp.int32), 0), axis=-1)
    return (chosen, picked)


def frame_sims(query_mat, ref_mat, regions):
    products = lax.dot_general(
        query_mat, ref_mat, (((1,), (1,)), ((), ())), preferred_element_type=jnp.float32
    )
    frames = query_mat.shape[0] // regions
    others = ref_mat.shape[0] // regions
    best = jnp.max(products.reshape(frames, regions, others, regions), axis=3)
    return jnp.sum(best, axis=1) * (1.0 / (regions * math.sqrt(query_mat.shape[1])))


def conv_layer(padded, weights, bias, block_rows, use_pool):
    channels = padded.shape[0]
    height = padded.shape[1] - 2
    width = padded.shape[2] - 2
    block_rows = math.gcd(height, block_rows)
    outputs = weights.shape[0]
    accuracy = lax.Precision.HIGHEST if padded.dtype == jnp.float32 else None

    def one_block(position):
        window = lax.dynamic_slice_in_dim(padded, position * block_rows, block_rows + 2, 1)
        stacked = jnp.concatenate(
            [
                window[:, shift_row : shift_row + block_rows, shift_col : shift_col + width]
                for shift_row in range(3)
                for shift_col in range(3)
            ],
            axis=0,
        )
        result = jnp.dot(
            weights,
            stacked.reshape(9 * channels, block_rows * width),
            preferred_element_type=jnp.float32,
            precision=accuracy,
        )
        result = (result + bias[:, None]).reshape(outputs, block_rows, width)
        result = jnp.maximum(result, 0.0)
        if use_pool:
            result = jnp.max(
                result.reshape(outputs, block_rows // 2, 2, width // 2, 2), axis=(2, 4)
            )
        return result

    blocks = lax.map(one_block, jnp.arange(height // block_rows, dtype=jnp.int32))
    return jnp.transpose(blocks, (1, 0, 2, 3)).reshape(outputs, -1, blocks.shape[-1])


def weight_matrix(weight):
    return jnp.transpose(weight, (2, 0, 1, 3)).reshape(weight.shape[2], -1)


def body(
    query_feats,
    ref_feats,
    pair_table,
    lengths,
    query_len,
    conv1_weight,
    conv1_bias,
    conv2_weight,
    conv2_bias,
    conv3_weight,
    conv3_bias,
    conv4_weight,
    conv4_bias,
):
    qry_index = lax.axis_index("qry")
    ref_index = lax.axis_index("ref")
    frames = query_feats.shape[0]
    regions = query_feats.shape[1]
    channels = query_feats.shape[2]
    tiles_here = pair_table.shape[1] // lax.axis_size("ref")
    tile_rows = ref_feats.shape[0] // tiles_here
    query_mat = query_feats.reshape(frames * regions, channels)
    own_mask = lax.dynamic_slice(pair_table, (qry_index, ref_index * tiles_here), (1, tiles_here))[
        0
    ]
    chosen, picked = slot_table(own_mask, MOST)
    shards = lax.all_gather(ref_feats, "qry", axis=1, tiled=True)
    senders = shards.shape[1]
    sims = frame_sims(query_mat, shards.reshape(tile_rows * senders * regions, channels), regions)
    sims = sims.reshape(1, frames, tile_rows, senders)
    tile_sims = sims.reshape(MOST, frames, frames)
    placed = jnp.einsum(
        "st,sqf->qtf", chosen.astype(jnp.float32), tile_sims, precision=lax.Precision.HIGHEST
    )
    sim_map = placed.reshape(frames, tiles_here * frames)
    padded = padded_2(sim_map, (("qry", 0), ("ref", 1)), 1)
    first_weights = jnp.transpose(conv1_weight, (2, 0, 1)).reshape(conv1_weight.shape[2], 9)
    first = conv_layer(padded[None], first_weights, conv1_bias, 32, True).astype(jnp.bfloat16)
    padded = padded_2(first, (("qry", 1), ("ref", 2)), 1)
    second = conv_layer(padded, weight_matrix(conv2_weight), conv2_bias, 16, True).astype(
        jnp.bfloat16
    )
    padded = padded_2(second, (("qry", 1), ("ref", 2)), 1)
    third = conv_layer(padded, weight_matrix(conv3_weight), conv3_bias, 16, False).astype(
        jnp.bfloat16
    )
    map_rows = third.shape[1]
    map_cols = third.shape[2]
    score_map = (
        jnp.dot(
            conv4_weight[None],
            third.reshape(third.shape[0], -1),
            preferred_element_type=jnp.float32,
        ).reshape(map_rows, map_cols)
        + conv4_bias[0]
    )
    ends = jnp.cumsum(lengths)
    starts = ends - lengths
    column = ref_index * map_cols + jnp.arange(map_cols, dtype=jnp.int32)
    member = (column[:, None] >= starts[None, :]) & (column[:, None] < ends[None, :])
    peaks = jnp.max(jnp.where(member[None], score_map[:, :, None], -jnp.inf), axis=1)
    peaks = lax.pmax(peaks, "ref")
    row_ids = qry_index * map_rows + jnp.arange(map_rows, dtype=jnp.int32)
    partial_value = jnp.sum(jnp.where((row_ids < query_len[0])[:, None], peaks, 0.0), axis=0)
    totals = lax.psum(partial_value, "qry")
    return (score_map, totals / query_len[0].astype(jnp.float32))


def solution(mesh):
    placed = (
        P(("groups", "qry"), None, None),
        P(("groups", "ref"), "qry", None, None),
        P("groups", None),
        P("groups"),
        P("groups"),
        P(),
        P(),
        P(),
        P(),
        P(),
        P(),
        P(),
        P(),
    )
    return jax.shard_map(
        body,
        mesh=mesh,
        in_specs=placed,
        out_specs=(P(("groups", "qry"), "ref"), P("groups")),
        check_vma=False,
    )
```

profile of v0, /device:TPU:0, one launch (start us, length us, event | category | flops | bytes accessed | tf_op | source)
XLA Modules:
  0.0 248.4 jit_solution(3101193552977106752)
XLA Ops:
  7.2 0.7 all-gather.2.cloned.1.call-update
  7.9 1.3 dynamic_slice.23
  10.5 62.7 %all-gather.2.cloned.1.call-done = bf16[32,4,9,3840]{3,0,2,1:T(8,128)(2,1)} async-done(((bf16[32,1,9,3840]{3,0,2,1:T(8,128)(2,1)}), bf16[32,4,9,3840]{3,0,2,1:T(8,128)(2,1)}) %all-gather.2.cloned.1.call-update) | async-done | bytes 8847376 | tf_op jit(solution)/shard_map/all_gather | solution.py:109
  73.2 8.6 %copy.62 = bf16[32,4,9,3840]{3,1,0,2:T(4,128)(2,1)} copy(bf16[32,4,9,3840]{3,0,2,1:T(8,128)(2,1)} %all-gather.2.cloned.1.call-done) | data formatting | bytes 17694720 | tf_op jit(solution)/shard_map/all_gather | solution.py:109
  81.8 12.7 %reshape.195 = bf16[128,9,3840,1]{2,0,1,3:T(8,128)(2,1)} reshape(bf16[32,4,9,3840]{3,1,0,2:T(4,128)(2,1)} %copy.62) | data formatting | bytes 17694720 | tf_op jit(solution)/shard_map/dot_general | solution.py:33
  94.5 18.8 %fusion.7 = f32[128,9,128]{2,0,1:T(8,128)S(1)} fusion(bf16[128,9,3840,1]{2,0,1,3:T(8,128)(2,1)} %reshape.195, bf16[128,9,3840]{2,0,1:T(8,128)(2,1)} %param.19), kind=kOutput, calls=%fused_computation.40 | convolution fusion | flops 10193338368 | bytes 18284544 | tf_op jit(solution)/shard_map/dot_general | solution.py:33
  113.4 2.2 collective-permute-start
  115.6 1.3 collective-permute-start.1
  116.9 1.7 collective-permute-done.1
  118.7 3.4 %collective-permute-start.2 = (f32[130,1]{1,0:T(8,128)S(1)}, f32[130,1]{1,0:T(8,128)S(1)}, u32[]{:S(2)}, u32[]{:S(2)}) collective-permute-start(f32[130,1]{1,0:T(8,128)S(1)} %get-tuple-element.223), channel_id=1, source_target_pairs={{0,1},{1,2},{2,3},{4,5},{5,6},{6,7},{8,9},{9,10},{10,11},{12,13},{... | collective-permute-start | bytes 1568 | tf_op jit(solution)/shard_map/ppermute | solution.py:15
  122.1 1.3 collective-permute-start.3
  124.1 4.3 %collective-permute-done.3 = f32[130,1]{1,0:T(8,128)S(1)} collective-permute-done((f32[130,1]{1,0:T(8,128)S(1)}, f32[130,1]{1,0:T(8,128)S(1)}, u32[]{:S(2)}, u32[]{:S(2)}) %collective-permute-start.3) | collective-permute-done | bytes 552 | tf_op jit(solution)/shard_map/ppermute | solution.py:18
  128.5 23.2 %while.30 = (s32[]{:T(128)}, bf16[4,32,16,64]{3,2,0,1:T(8,128)(2,1)S(1)}, s32[4]{0:T(128)S(1)}, f32[1,130,130]{2,1,0:T(8,128)S(1)}, f32[32,9]{0,1:T(8,128)S(1)},...) while((s32[]{:T(128)}, ...), condition=%wide.region_4.5_spmd, body=%wide.region_2.4_spmd.sunk | while | flops 14647306 | bytes 2885173 | solution.py:74
  128.5 0.6 dynamic_slice.27
  130.5 0.6 fusion.36
  131.6 2.5 %reduce_max.42 = bf16[32,16,64]{0,2,1:T(8,128)(2,1)S(1)} reduce(bf16[32,16,2,64,2]{0,4,3,2,1:T(2,128)(2,1)S(1)} %bitcast.115, bf16[]{:T(256)} %constant.179..sunk), dimensions={2,4}, to_apply=%region_3.3 | reduce | flops 98304 | bytes 327682 | tf_op jit(solution)/shard_map/while/body/eval_jaxpr/reduce_max | solution.py:69
  134.3 0.6 dynamic_slice.27
  136.3 0.6 fusion.36
  137.4 2.5 %reduce_max.42 = bf16[32,16,64]{0,2,1:T(8,128)(2,1)S(1)} reduce(bf16[32,16,2,64,2]{0,4,3,2,1:T(2,128)(2,1)S(1)} %bitcast.115, bf16[]{:T(256)} %constant.179..sunk), dimensions={2,4}, to_apply=%region_3.3 | reduce | flops 98304 | bytes 327682 | tf_op jit(solution)/shard_map/while/body/eval_jaxpr/reduce_max | solution.py:69
  140.1 0.6 dynamic_slice.27
  142.1 0.6 fusion.36
  143.2 2.5 %reduce_max.42 = bf16[32,16,64]{0,2,1:T(8,128)(2,1)S(1)} reduce(bf16[32,16,2,64,2]{0,4,3,2,1:T(2,128)(2,1)S(1)} %bitcast.115, bf16[]{:T(256)} %constant.179..sunk), dimensions={2,4}, to_apply=%region_3.3 | reduce | flops 98304 | bytes 327682 | tf_op jit(solution)/shard_map/while/body/eval_jaxpr/reduce_max | solution.py:69
  145.9 0.6 dynamic_slice.27
  147.9 0.6 fusion.36
  149.0 2.5 %reduce_max.42 = bf16[32,16,64]{0,2,1:T(8,128)(2,1)S(1)} reduce(bf16[32,16,2,64,2]{0,4,3,2,1:T(2,128)(2,1)S(1)} %bitcast.115, bf16[]{:T(256)} %constant.179..sunk), dimensions={2,4}, to_apply=%region_3.3 | reduce | flops 98304 | bytes 327682 | tf_op jit(solution)/shard_map/while/body/eval_jaxpr/reduce_max | solution.py:69
  151.7 2.7 %collective-permute-start.4 = (bf16[32,1,64]{2,1,0:T(2,128)(2,1)S(1)}, bf16[32,1,64]{2,1,0:T(2,128)(2,1)S(1)}, u32[]{:S(2)}, u32[]{:S(2)}) collective-permute-start(bf16[32,1,64]{2,1,0:T(2,128)(2,1)S(1)} %get-tuple-element.217), channel_id=1, source_target_pairs={{0,4},{4,8},{8,12},{1,5},{5,9},{9,13},{2,6},{6,10},{10,14},{3,7},{... | collective-permute-start | bytes 12296 | tf_op jit(solution)/shard_map/ppermute | solution.py:15
  154.5 1.3 collective-permute-start.5
  155.8 2.7 %collective-permute-done.5 = bf16[32,1,64]{2,1,0:T(2,128)(2,1)S(1)} collective-permute-done((bf16[32,1,64]{2,1,0:T(2,128)(2,1)S(1)}, bf16[32,1,64]{2,1,0:T(2,128)(2,1)S(1)}, u32[]{:S(2)}, u32[]{:S(2)}) %collective-permute-start.5) | collective-permute-done | bytes 4128 | tf_op jit(solution)/shard_map/ppermute | solution.py:18
  159.3 3.4 %collective-permute-start.6 = (bf16[32,66,1]{1,0,2:T(8,128)(2,1)S(1)}, bf16[32,66,1]{1,0,2:T(8,128)(2,1)S(1)}, u32[]{:S(2)}, u32[]{:S(2)}) collective-permute-start(bf16[32,66,1]{1,0,2:T(8,128)(2,1)S(1)} %copy.64), channel_id=1, source_target_pairs={{0,1},{1,2},{2,3},{4,5},{5,6},{6,7},{8,9},{9,10},{10,11},{12,13},{... | collective-permute-start | bytes 12680 | tf_op jit(solution)/shard_map/ppermute | solution.py:15
  163.1 1.5 collective-permute-start.7
  164.8 0.9 copy.66
  165.7 2.9 %collective-permute-done.7 = bf16[32,66,1]{1,0,2:T(8,128)(2,1)S(1)} collective-permute-done((bf16[32,66,1]{1,0,2:T(8,128)(2,1)S(1)}, bf16[32,66,1]{1,0,2:T(8,128)(2,1)S(1)}, u32[]{:S(2)}, u32[]{:S(2)}) %collective-permute-start.7) | collective-permute-done | bytes 4256 | tf_op jit(solution)/shard_map/ppermute | solution.py:18
  168.6 0.9 copy.68
  170.1 32.3 %while.31 = (s32[]{:T(128)}, bf16[4,64,8,32]{1,3,2,0:T(8,128)(2,1)}, s32[4]{0:T(128)S(1)}, bf16[32,66,66]{2,0,1:T(8,128)(2,1)S(1)}, bf16[64,288]{1,0:T(8,128)(2,...) while((s32[]{:T(128)}, ...), condition=%wide.region_7.8_spmd, body=%wide.region_5.7_spmd.sunk | while | flops 37994504 | bytes 4822013 | solution.py:74
  170.1 0.6 dynamic_slice.28
  173.1 0.8 copy.113
  174.0 2.4 concatenate.35
  177.0 0.6 reduce_max.43
  177.6 0.6 bitcast_dynamic-update-slice_fusion.2
  181.2 0.8 copy.113
  182.1 2.4 concatenate.35
  185.0 0.6 reduce_max.43
  185.6 0.6 bitcast_dynamic-update-slice_fusion.2
  189.3 0.8 copy.113
  190.1 2.4 concatenate.35
  193.1 0.6 reduce_max.43
  193.7 0.6 bitcast_dynamic-update-slice_fusion.2
  197.4 0.8 copy.113
  198.2 2.4 concatenate.35
  201.2 0.6 reduce_max.43
  201.8 0.6 bitcast_dynamic-update-slice_fusion.2
  202.4 0.7 fusion.14
  203.1 2.9 %collective-permute-start.8 = (bf16[64,1,32]{0,2,1:T(8,128)(2,1)S(1)}, bf16[64,1,32]{0,2,1:T(8,128)(2,1)S(1)}, u32[]{:S(2)}, u32[]{:S(2)}) collective-permute-start(bf16[64,1,32]{0,2,1:T(8,128)(2,1)S(1)} %get-tuple-element.221), channel_id=1, source_target_pairs={{0,4},{4,8},{8,12},{1,5},{5,9},{9,13},{2,6},{6,10},{10,14},{3,7},{... | collective-permute-start | bytes 12296 | tf_op jit(solution)/shard_map/ppermute | solution.py:15
  206.1 1.3 collective-permute-start.9
  208.1 2.0 collective-permute-done.9
  210.1 0.9 pad_maximum_fusion.6
  211.0 3.4 %collective-permute-start.10 = (bf16[64,34,1]{0,2,1:T(2,128)(2,1)S(1)}, bf16[64,34,1]{0,2,1:T(2,128)(2,1)S(1)}, u32[]{:S(2)}, u32[]{:S(2)}) collective-permute-start(bf16[64,34,1]{0,2,1:T(2,128)(2,1)S(1)} %get-tuple-element.219), channel_id=1, source_target_pairs={{0,1},{1,2},{2,3},{4,5},{5,6},{6,7},{8,9},{9,10},{10,11},{12,13},{... | collective-permute-start | bytes 13064 | tf_op jit(solution)/shard_map/ppermute | solution.py:15
  214.4 1.3 collective-permute-start.11
  215.8 1.1 copy.71
  217.5 2.6 %collective-permute-done.11 = bf16[64,34,1]{0,2,1:T(2,128)(2,1)S(1)} collective-permute-done((bf16[64,34,1]{0,2,1:T(2,128)(2,1)S(1)}, bf16[64,34,1]{0,2,1:T(2,128)(2,1)S(1)}, u32[]{:S(2)}, u32[]{:S(2)}) %collective-permute-start.11) | collective-permute-done | bytes 4384 | tf_op jit(solution)/shard_map/ppermute | solution.py:18
  220.1 1.1 pad_maximum_fusion.2
  221.2 4.8 %while.32 = (s32[]{:T(128)}, bf16[2,128,16,32]{1,3,2,0:T(8,128)(2,1)S(1)}, s32[2]{0:T(128)S(1)}, bf16[64,34,34]{0,2,1:T(8,128)(2,1)S(1)}, bf16[128,576]{1,0:T(8,...) while((s32[]{:T(128)}, ...), condition=%wide.region_9.10_spmd, body=%wide.region_8.9_spmd.sunk | while | flops 75694088 | bytes 3490551 | solution.py:74
  226.6 8.5 %pmax.7 = f32[32,2]{0,1:T(2,128)S(1)} all-reduce(f32[32,2]{0,1:T(2,128)S(1)} %select_reduce_fusion), channel_id=1, replica_groups=mesh['groups'=2,'qry'=4,'ref'=4] {'ref'}, use_global_device_ids=true, to_apply=%region_12.13 | all-reduce | flops 64 | bytes 512 | tf_op jit(solution)/shard_map/pmax | solution.py:144
  235.2 5.8 %psum.7 = f32[2]{0:T(128)S(1)} all-reduce(f32[2]{0:T(128)S(1)} %select_reduce_fusion.1), channel_id=1, replica_groups=mesh['groups'=2,'qry'=4,'ref'=4] {'qry'}, use_global_device_ids=true, to_apply=%region_14.15 | all-reduce | flops 2 | bytes 16 | tf_op jit(solution)/shard_map/psum | solution.py:147
  (167 shorter events, 23.9 us)
Async XLA Ops:
  7.2 218.9 %copy-start = (bf16[128]{0:T(256)(128)(2,1)S(1)}, bf16[128]{0:T(256)(128)(2,1)}, u32[]{:S(2)}) copy-start(bf16[128]{0:T(256)(128)(2,1)} %param.30) | copy-start | bytes 772
  7.2 66.0 %all-gather.2.cloned.1.call-start = ((), (), s32[]{:S(2)}) async-start(), calls=%async_computation | async-start | bytes 11059200 | tf_op jit(solution)/shard_map/all_gather | solution.py:109
  94.5 28.9 %copy-start.6 = (f32[3,3,32]{2,1,0:T(4,128)S(1)}, f32[3,3,32]{2,1,0:T(4,128)}, u32[]{:S(2)}) copy-start(f32[3,3,32]{2,1,0:T(4,128)} %param.24) | copy-start | bytes 3460
  94.5 29.0 %copy-start.7 = (s32[2]{0:T(128)S(1)}, s32[2]{0:T(128)}, u32[]{:S(2)}) copy-start(s32[2]{0:T(128)} %param.22) | copy-start | bytes 28
  94.5 34.0 %copy-start.5 = (f32[32]{0:T(128)S(1)}, f32[32]{0:T(128)}, u32[]{:S(2)}) copy-start(f32[32]{0:T(128)} %param.25) | copy-start | bytes 388
  113.4 3.5 %collective-permute-start = (f32[1,128]{1,0:T(1,128)S(1)}, f32[1,128]{1,0:T(1,128)S(1)}, u32[]{:S(2)}, u32[]{:S(2)}) collective-permute-start(f32[1,128]{1,0:T(1,128)S(1)} %get-tuple-element.225), channel_id=1, source_target_pairs={{0,4},{4,8},{8,12},{1,5},{5,9},{9,13},{2,6},{6,10},{10,14},{3,7},{... | collective-permute-start | bytes 1544 | tf_op jit(solution)/shard_map/ppermute | solution.py:15
  115.6 3.1 %collective-permute-start.1 = (f32[1,128]{1,0:T(1,128)S(1)}, f32[1,128]{1,0:T(1,128)S(1)}, u32[]{:S(2)}, u32[]{:S(2)}) collective-permute-start(f32[1,128]{1,0:T(1,128)S(1)} %get-tuple-element.226), channel_id=1, source_target_pairs={{4,0},{8,4},{12,8},{5,1},{9,5},{13,9},{6,2},{10,6},{14,10},{7,3},{... | collective-permute-start | bytes 1544 | tf_op jit(solution)/shard_map/ppermute | solution.py:18
  118.7 5.3 %collective-permute-start.2 = (f32[130,1]{1,0:T(8,128)S(1)}, f32[130,1]{1,0:T(8,128)S(1)}, u32[]{:S(2)}, u32[]{:S(2)}) collective-permute-start(f32[130,1]{1,0:T(8,128)S(1)} %get-tuple-element.223), channel_id=1, source_target_pairs={{0,1},{1,2},{2,3},{4,5},{5,6},{6,7},{8,9},{9,10},{10,11},{12,13},{... | collective-permute-start | bytes 1568 | tf_op jit(solution)/shard_map/ppermute | solution.py:15
  122.1 6.2 %collective-permute-start.3 = (f32[130,1]{1,0:T(8,128)S(1)}, f32[130,1]{1,0:T(8,128)S(1)}, u32[]{:S(2)}, u32[]{:S(2)}) collective-permute-start(f32[130,1]{1,0:T(8,128)S(1)} %get-tuple-element.224), channel_id=1, source_target_pairs={{1,0},{2,1},{3,2},{5,4},{6,5},{7,6},{9,8},{10,9},{11,10},{13,12},{... | collective-permute-start | bytes 1568 | tf_op jit(solution)/shard_map/ppermute | solution.py:18
  128.5 36.1 %copy-start.1 = (bf16[3,3,64,32]{2,3,1,0:T(8,128)(2,1)S(1)}, bf16[3,3,64,32]{2,3,1,0:T(8,128)(2,1)}, u32[]{:S(2)}) copy-start(bf16[3,3,64,32]{2,3,1,0:T(8,128)(2,1)} %param.26) | copy-start | bytes 110596
  151.7 18.4 %copy-start.3 = (f32[64]{0:T(128)S(1)}, f32[64]{0:T(128)}, u32[]{:S(2)}) copy-start(f32[64]{0:T(128)} %param.27) | copy-start | bytes 772
  151.7 4.1 %collective-permute-start.4 = (bf16[32,1,64]{2,1,0:T(2,128)(2,1)S(1)}, bf16[32,1,64]{2,1,0:T(2,128)(2,1)S(1)}, u32[]{:S(2)}, u32[]{:S(2)}) collective-permute-start(bf16[32,1,64]{2,1,0:T(2,128)(2,1)S(1)} %get-tuple-element.217), channel_id=1, source_target_pairs={{0,4},{4,8},{8,12},{1,5},{5,9},{9,13},{2,6},{6,10},{10,14},{3,7},{... | collective-permute-start | bytes 12296 | tf_op jit(solution)/shard_map/ppermute | solution.py:15
  154.5 4.1 %collective-permute-start.5 = (bf16[32,1,64]{2,1,0:T(2,128)(2,1)S(1)}, bf16[32,1,64]{2,1,0:T(2,128)(2,1)S(1)}, u32[]{:S(2)}, u32[]{:S(2)}) collective-permute-start(bf16[32,1,64]{2,1,0:T(2,128)(2,1)S(1)} %get-tuple-element.218), channel_id=1, source_target_pairs={{4,0},{8,4},{12,8},{5,1},{9,5},{13,9},{6,2},{10,6},{14,10},{7,3},{... | collective-permute-start | bytes 12296 | tf_op jit(solution)/shard_map/ppermute | solution.py:18
  159.3 5.4 %collective-permute-start.6 = (bf16[32,66,1]{1,0,2:T(8,128)(2,1)S(1)}, bf16[32,66,1]{1,0,2:T(8,128)(2,1)S(1)}, u32[]{:S(2)}, u32[]{:S(2)}) collective-permute-start(bf16[32,66,1]{1,0,2:T(8,128)(2,1)S(1)} %copy.64), channel_id=1, source_target_pairs={{0,1},{1,2},{2,3},{4,5},{5,6},{6,7},{8,9},{9,10},{10,11},{12,13},{... | collective-permute-start | bytes 12680 | tf_op jit(solution)/shard_map/ppermute | solution.py:15
  163.1 5.5 %collective-permute-start.7 = (bf16[32,66,1]{1,0,2:T(8,128)(2,1)S(1)}, bf16[32,66,1]{1,0,2:T(8,128)(2,1)S(1)}, u32[]{:S(2)}, u32[]{:S(2)}) collective-permute-start(bf16[32,66,1]{1,0,2:T(8,128)(2,1)S(1)} %copy.65), channel_id=1, source_target_pairs={{1,0},{2,1},{3,2},{5,4},{6,5},{7,6},{9,8},{10,9},{11,10},{13,12},{... | collective-permute-start | bytes 12680 | tf_op jit(solution)/shard_map/ppermute | solution.py:18
  170.1 51.1 %copy-start.4 = (f32[128]{0:T(128)S(1)}, f32[128]{0:T(128)}, u32[]{:S(2)}) copy-start(f32[128]{0:T(128)} %param.29) | copy-start | bytes 1540
  203.1 5.0 %collective-permute-start.8 = (bf16[64,1,32]{0,2,1:T(8,128)(2,1)S(1)}, bf16[64,1,32]{0,2,1:T(8,128)(2,1)S(1)}, u32[]{:S(2)}, u32[]{:S(2)}) collective-permute-start(bf16[64,1,32]{0,2,1:T(8,128)(2,1)S(1)} %get-tuple-element.221), channel_id=1, source_target_pairs={{0,4},{4,8},{8,12},{1,5},{5,9},{9,13},{2,6},{6,10},{10,14},{3,7},{... | collective-permute-start | bytes 12296 | tf_op jit(solution)/shard_map/ppermute | solution.py:15
  206.1 4.0 %collective-permute-start.9 = (bf16[64,1,32]{0,2,1:T(8,128)(2,1)S(1)}, bf16[64,1,32]{0,2,1:T(8,128)(2,1)S(1)}, u32[]{:S(2)}, u32[]{:S(2)}) collective-permute-start(bf16[64,1,32]{0,2,1:T(8,128)(2,1)S(1)} %get-tuple-element.222), channel_id=1, source_target_pairs={{4,0},{8,4},{12,8},{5,1},{9,5},{13,9},{6,2},{10,6},{14,10},{7,3},{... | collective-permute-start | bytes 12296 | tf_op jit(solution)/shard_map/ppermute | solution.py:18
  211.0 6.5 %collective-permute-start.10 = (bf16[64,34,1]{0,2,1:T(2,128)(2,1)S(1)}, bf16[64,34,1]{0,2,1:T(2,128)(2,1)S(1)}, u32[]{:S(2)}, u32[]{:S(2)}) collective-permute-start(bf16[64,34,1]{0,2,1:T(2,128)(2,1)S(1)} %get-tuple-element.219), channel_id=1, source_target_pairs={{0,1},{1,2},{2,3},{4,5},{5,6},{6,7},{8,9},{9,10},{10,11},{12,13},{... | collective-permute-start | bytes 13064 | tf_op jit(solution)/shard_map/ppermute | solution.py:15
  214.4 5.6 %collective-permute-start.11 = (bf16[64,34,1]{0,2,1:T(2,128)(2,1)S(1)}, bf16[64,34,1]{0,2,1:T(2,128)(2,1)S(1)}, u32[]{:S(2)}, u32[]{:S(2)}) collective-permute-start(bf16[64,34,1]{0,2,1:T(2,128)(2,1)S(1)} %get-tuple-element.220), channel_id=1, source_target_pairs={{1,0},{2,1},{3,2},{5,4},{6,5},{7,6},{9,8},{10,9},{11,10},{13,12},{... | collective-permute-start | bytes 13064 | tf_op jit(solution)/shard_map/ppermute | solution.py:18
  226.5 15.1 %copy-start.2 = (f32[32,32]{1,0:T(8,128)}, f32[32,32]{1,0:T(8,128)S(1)}, u32[]{:S(2)}) copy-start(f32[32,32]{1,0:T(8,128)S(1)} %broadcast_add_fusion) | copy-start | bytes 12292
Sparse Core Ops, SparseCore 0:
  9.5 63.5 all-gather.1
where the time goes:
time: 250 us; the launch traced here: 248 us
  waiting for transfers between devices  80 us (32%)
  local copies, waits for them, and re-layouts  63.7 us (25%)
  starting transfers between devices  26 us (10%)
  matrix products  23.9 us (10%)
  between operations  17.1 us (7%)
  other arithmetic  16.3 us (7%)
  blocking collectives  14.3 us (6%)
  loops' own time  7.15 us (3%)
    all_gather x1, waiting for transfers between devices, body(): shards = lax.all_gather(ref_feats, 'qry', axis=1, tiled=True)  62.7 us
    dot_general x1, matrix products, frame_sims(): lax.dot_general(query_mat, ref_mat, (((1,), (1,)), ((), ())), preferred_e...  18.8 us
    ppermute x6, starting transfers between devices, padded_2(): lax.ppermute(lax.slice_in_dim(block, block.shape[dim] - width, None, axis...  18 us
    ppermute x6, waiting for transfers between devices, padded_2(): lax.ppermute(lax.slice_in_dim(block, 0, width, axis=dim), axis, backward)  16.2 us
    dot_general x1, local copies, waits for them, and re-layouts, frame_sims(): lax.dot_general(query_mat, ref_mat, (((1,), (1,)), ((), ())), preferred_e...  12.7 us
    reduce_max x8, other arithmetic, one_block(): jnp.max(result.reshape(outputs, block_rows // 2, 2, width // 2, 2), axis=...  12.3 us
    while x76, local copies, waits for them, and re-layouts  11.5 us
    concatenate x10, local copies, waits for them, and re-layouts, one_block(): jnp.concatenate([window[:, shift_row:shift_row + block_rows, shift_col:sh...  11 us
  transfers between devices with their start and end apart: 13, of which 8 were waited for; matrix products, arithmetic and copies ran while one was open for 2% of the time, Pallas kernels for 0%

commit v1 on v0

--- a/solution.py
+++ b/solution.py
@@ -106,7 +106,9 @@
         0
     ]
     chosen, picked = slot_table(own_mask, MOST)
-    shards = lax.all_gather(ref_feats, "qry", axis=1, tiled=True)
+    shards = jnp.concatenate(
+        lax.all_to_all(jnp.stack([ref_feats] * lax.axis_size("qry")), "qry", 0, 0), axis=1
+    )
     senders = shards.shape[1]
     sims = frame_sims(query_mat, shards.reshape(tile_rows * senders * regions, channels), regions)
     sims = sims.reshape(1, frames, tile_rows, senders)

time: 250 us -> 283 us (1.13)
  waiting for transfers between devices: 80 us -> 113 us
  between operations: 17.1 us -> 3.67 us
  local copies, waits for them, and re-layouts: 63.7 us -> 70.2 us
  starting transfers between devices: 26 us -> 32.4 us
    all_to_all x0 -> x1, waiting for transfers between devices: none -> 96.2 us  [body(): lax.all_to_all(jnp.stack([ref_feats] * lax.axis_size('qry')), 'qry', 0, 0)]
    all_gather x1 -> x0, waiting for transfers between devices: 62.7 us -> none  [body(): shards = lax.all_gather(ref_feats, 'qry', axis=1, tiled=True)]
    reshape x0 -> x1, local copies, waits for them, and re-layouts: none -> 8.66 us  [body(): jnp.concatenate(lax.all_to_all(jnp.stack([ref_feats] * lax.axis_size('qry...]
    all_gather x1 -> x0, local copies, waits for them, and re-layouts: 8.6 us -> none  [body(): shards = lax.all_gather(ref_feats, 'qry', axis=1, tiled=True)]
    another operation x0 -> x1, local copies, waits for them, and re-layouts: none -> 6.12 us  [body(): jnp.stack([ref_feats] * lax.axis_size('qry'))]
    all_to_all x0 -> x1, starting transfers between devices: none -> 5.7 us  [body(): lax.all_to_all(jnp.stack([ref_feats] * lax.axis_size('qry')), 'qry', 0, 0)]
  transfers between devices with their start and end apart: 13 -> 13, of which waited for: 8 -> 8; matrix products, arithmetic and copies ran while one was open for 2% -> 1% of each run, Pallas kernels for 0% -> 0%
where the time goes in v1:
time: 283 us; the launch traced here: 281 us
  waiting for transfers between devices  113 us (40%)
  local copies, waits for them, and re-layouts  70.2 us (25%)
  starting transfers between devices  32.4 us (11%)
  matrix products  23.9 us (8%)
  other arithmetic  16.3 us (6%)
  blocking collectives  14.3 us (5%)
  loops' own time  7.39 us (3%)
  between operations  3.67 us (1%)
    all_to_all x1, waiting for transfers between devices, body(): lax.all_to_all(jnp.stack([ref_feats] * lax.axis_size('qry')), 'qry', 0, 0)  96.2 us
    dot_general x1, matrix products, frame_sims(): lax.dot_general(query_mat, ref_mat, (((1,), (1,)), ((), ())), preferred_e...  18.8 us
    ppermute x6, starting transfers between devices, padded_2(): lax.ppermute(lax.slice_in_dim(block, block.shape[dim] - width, None, axis...  18.8 us
    ppermute x6, waiting for transfers between devices, padded_2(): lax.ppermute(lax.slice_in_dim(block, 0, width, axis=dim), axis, backward)  16.2 us
    dot_general x1, local copies, waits for them, and re-layouts, frame_sims(): lax.dot_general(query_mat, ref_mat, (((1,), (1,)), ((), ())), preferred_e...  12.8 us
    reduce_max x8, other arithmetic, one_block(): jnp.max(result.reshape(outputs, block_rows // 2, 2, width // 2, 2), axis=...  12.3 us
    while x76, local copies, waits for them, and re-layouts  11.5 us
    concatenate x10, local copies, waits for them, and re-layouts, one_block(): jnp.concatenate([window[:, shift_row:shift_row + block_rows, shift_col:sh...  11 us
  transfers between devices with their start and end apart: 13, of which 8 were waited for; matrix products, arithmetic and copies ran while one was open for 1% of the time, Pallas kernels for 0%

profile of v1, /device:TPU:0, one launch (start us, length us, event | category | flops | bytes accessed | tf_op | source)
XLA Modules:
  0.0 281.1 jit_solution(12097397099688447556)
XLA Ops:
  0.6 6.1 %stack.2 = bf16[4,32,1,9,3840]{4,1,3,2,0:T(8,128)(2,1)} broadcast(bf16[32,9,3840]{2,0,1:T(8,128)(2,1)} %bitcast.125), dimensions={1,3,4} | broadcast | bytes 11059200 | tf_op jit(solution)/shard_map/stack | solution.py:110
  6.8 5.7 %all-to-all-start = ((bf16[4,32,1,9,3840]{4,1,3,2,0:T(8,128)(2,1)}), bf16[4,32,1,9,3840]{4,1,3,2,0:T(8,128)(2,1)}, u32[]{:S(2)}, u32[]{:S(2)}) async-start(bf16[4,32,1,9,3840]{4,1,3,2,0:T(8,128)(2,1)} %stack.2), calls=%async_computation | async-start | bytes 17694720 | tf_op jit(solution)/shard_map/all_to_all | solution.py:110
  12.5 1.3 dynamic_slice.23
  15.1 96.2 %all-to-all-done = bf16[4,32,1,9,3840]{4,1,3,2,0:T(8,128)(2,1)} async-done(((bf16[4,32,1,9,3840]{4,1,3,2,0:T(8,128)(2,1)}), bf16[4,32,1,9,3840]{4,1,3,2,0:T(8,128)(2,1)}, u32[]{:S(2)}, u32[]{:S(2)}) %all-to-all-start) | async-done | bytes 8847392 | tf_op jit(solution)/shard_map/all_to_all | solution.py:110
  111.3 8.7 %copy.60 = bf16[32,4,1,9,3840]{4,1,0,3,2:T(4,128)(2,1)} copy(bf16[32,4,1,9,3840]{4,0,3,2,1:T(8,128)(2,1)} %bitcast.16) | data formatting | bytes 17694720 | tf_op jit(solution)/shard_map/reshape | solution.py:109
  119.9 12.8 %reshape.201 = bf16[128,9,3840,1]{2,0,1,3:T(8,128)(2,1)} reshape(bf16[32,4,1,9,3840]{4,1,0,3,2:T(4,128)(2,1)} %copy.60) | data formatting | bytes 17694720 | tf_op jit(solution)/shard_map/dot_general | solution.py:33
  132.7 18.8 %fusion.7 = f32[128,9,128]{2,0,1:T(8,128)S(1)} fusion(bf16[128,9,3840,1]{2,0,1,3:T(8,128)(2,1)} %reshape.201, bf16[128,9,3840]{2,0,1:T(8,128)(2,1)} %param.19), kind=kOutput, calls=%fused_computation.40 | convolution fusion | flops 10193338368 | bytes 18284544 | tf_op jit(solution)/shard_map/dot_general | solution.py:33
  151.6 1.3 collective-permute-start
  152.9 1.3 collective-permute-start.1
  154.3 1.7 collective-permute-done.1
  156.1 4.8 %collective-permute-start.2 = (f32[130,1]{1,0:T(8,128)S(1)}, f32[130,1]{1,0:T(8,128)S(1)}, u32[]{:S(2)}, u32[]{:S(2)}) collective-permute-start(f32[130,1]{1,0:T(8,128)S(1)} %get-tuple-element.223), channel_id=1, source_target_pairs={{0,1},{1,2},{2,3},{4,5},{5,6},{6,7},{8,9},{9,10},{10,11},{12,13},{... | collective-permute-start | bytes 1568 | tf_op jit(solution)/shard_map/ppermute | solution.py:15
  160.9 1.3 collective-permute-start.3
  162.9 4.3 %collective-permute-done.3 = f32[130,1]{1,0:T(8,128)S(1)} collective-permute-done((f32[130,1]{1,0:T(8,128)S(1)}, f32[130,1]{1,0:T(8,128)S(1)}, u32[]{:S(2)}, u32[]{:S(2)}) %collective-permute-start.3) | collective-permute-done | bytes 552 | tf_op jit(solution)/shard_map/ppermute | solution.py:18
  167.3 23.2 %while.30 = (s32[]{:T(128)}, bf16[4,32,16,64]{3,2,0,1:T(8,128)(2,1)S(1)}, s32[4]{0:T(128)S(1)}, f32[1,130,130]{2,1,0:T(8,128)S(1)}, f32[32,9]{0,1:T(8,128)S(1)},...) while((s32[]{:T(128)}, ...), condition=%wide.region_4.5_spmd, body=%wide.region_2.4_spmd.sunk | while | flops 14647306 | bytes 2885173 | solution.py:74
  167.3 0.6 dynamic_slice.27
  169.3 0.6 fusion.36
  170.4 2.5 reduce_max.42
  175.1 0.6 fusion.36
  176.2 2.5 reduce_max.42
  180.9 0.6 fusion.36
  182.0 2.5 reduce_max.42
  186.7 0.6 fusion.36
  187.8 2.5 reduce_max.42
  190.5 2.8 collective-permute-start.4
  193.3 1.3 collective-permute-start.5
  194.7 2.7 collective-permute-done.5
  198.2 3.5 %collective-permute-start.6 = (bf16[32,66,1]{1,0,2:T(8,128)(2,1)S(1)}, bf16[32,66,1]{1,0,2:T(8,128)(2,1)S(1)}, u32[]{:S(2)}, u32[]{:S(2)}) collective-permute-start(bf16[32,66,1]{1,0,2:T(8,128)(2,1)S(1)} %copy.62), channel_id=1, source_target_pairs={{0,1},{1,2},{2,3},{4,5},{5,6},{6,7},{8,9},{9,10},{10,11},{12,13},{... | collective-permute-start | bytes 12680 | tf_op jit(solution)/shard_map/ppermute | solution.py:15
  202.0 1.5 collective-permute-start.7
  203.7 0.9 copy.64
  204.7 2.9 %collective-permute-done.7 = bf16[32,66,1]{1,0,2:T(8,128)(2,1)S(1)} collective-permute-done((bf16[32,66,1]{1,0,2:T(8,128)(2,1)S(1)}, bf16[32,66,1]{1,0,2:T(8,128)(2,1)S(1)}, u32[]{:S(2)}, u32[]{:S(2)}) %collective-permute-start.7) | collective-permute-done | bytes 4256 | tf_op jit(solution)/shard_map/ppermute | solution.py:18
  207.6 0.9 copy.66
  209.0 32.4 %while.31 = (s32[]{:T(128)}, bf16[4,64,8,32]{1,3,2,0:T(8,128)(2,1)}, s32[4]{0:T(128)S(1)}, bf16[32,66,66]{2,0,1:T(8,128)(2,1)S(1)}, bf16[64,288]{1,0:T(8,128)(2,...) while((s32[]{:T(128)}, ...), condition=%wide.region_7.8_spmd, body=%wide.region_5.7_spmd.sunk | while | flops 37994504 | bytes 4822013 | solution.py:74
  209.1 0.6 dynamic_slice.28
  212.1 0.8 copy.111
  212.9 2.4 concatenate.35
  215.9 0.6 reduce_max.43
  216.5 0.6 bitcast_dynamic-update-slice_fusion.2
  220.2 0.8 copy.111
  221.0 2.4 concatenate.35
  224.0 0.6 reduce_max.43
  224.6 0.6 bitcast_dynamic-update-slice_fusion.2
  228.3 0.8 copy.111
  229.1 2.4 concatenate.35
  232.1 0.6 reduce_max.43
  232.7 0.6 bitcast_dynamic-update-slice_fusion.2
  236.3 0.8 copy.111
  237.2 2.4 concatenate.35
  240.2 0.6 reduce_max.43
  240.8 0.6 bitcast_dynamic-update-slice_fusion.2
  241.4 0.7 fusion.14
  242.1 2.9 %collective-permute-start.8 = (bf16[64,1,32]{0,2,1:T(8,128)(2,1)S(1)}, bf16[64,1,32]{0,2,1:T(8,128)(2,1)S(1)}, u32[]{:S(2)}, u32[]{:S(2)}) collective-permute-start(bf16[64,1,32]{0,2,1:T(8,128)(2,1)S(1)} %get-tuple-element.221), channel_id=1, source_target_pairs={{0,4},{4,8},{8,12},{1,5},{5,9},{9,13},{2,6},{6,10},{10,14},{3,7},{... | collective-permute-start | bytes 12296 | tf_op jit(solution)/shard_map/ppermute | solution.py:15
  245.1 1.3 collective-permute-start.9
  247.1 2.0 collective-permute-done.9
  249.1 0.9 pad_maximum_fusion.6
  250.0 3.5 %collective-permute-start.10 = (bf16[64,34,1]{0,2,1:T(2,128)(2,1)S(1)}, bf16[64,34,1]{0,2,1:T(2,128)(2,1)S(1)}, u32[]{:S(2)}, u32[]{:S(2)}) collective-permute-start(bf16[64,34,1]{0,2,1:T(2,128)(2,1)S(1)} %get-tuple-element.219), channel_id=1, source_target_pairs={{0,1},{1,2},{2,3},{4,5},{5,6},{6,7},{8,9},{9,10},{10,11},{12,13},{... | collective-permute-start | bytes 13064 | tf_op jit(solution)/shard_map/ppermute | solution.py:15
  253.5 1.3 collective-permute-start.11
  254.8 1.1 copy.69
  256.5 2.6 collective-permute-done.11
  259.1 1.1 pad_maximum_fusion.2
  260.3 5.3 %while.32 = (s32[]{:T(128)}, bf16[2,128,16,32]{1,3,2,0:T(8,128)(2,1)S(1)}, s32[2]{0:T(128)S(1)}, bf16[64,34,34]{0,2,1:T(8,128)(2,1)S(1)}, bf16[128,576]{1,0:T(8,...) while((s32[]{:T(128)}, ...), condition=%wide.region_9.10_spmd, body=%wide.region_8.9_spmd.sunk | while | flops 75694088 | bytes 3490551 | solution.py:74
  260.3 0.7 dynamic_slice.29
  262.9 0.7 dynamic_slice.29
  266.1 8.5 %pmax.7 = f32[32,2]{0,1:T(2,128)S(1)} all-reduce(f32[32,2]{0,1:T(2,128)S(1)} %select_reduce_fusion), channel_id=1, replica_groups=mesh['groups'=2,'qry'=4,'ref'=4] {'ref'}, use_global_device_ids=true, to_apply=%region_12.13 | all-reduce | flops 64 | bytes 512 | tf_op jit(solution)/shard_map/pmax | solution.py:146
  274.7 5.8 %psum.7 = f32[2]{0:T(128)S(1)} all-reduce(f32[2]{0:T(128)S(1)} %select_reduce_fusion.1), channel_id=1, replica_groups=mesh['groups'=2,'qry'=4,'ref'=4] {'qry'}, use_global_device_ids=true, to_apply=%region_14.15 | all-reduce | flops 2 | bytes 16 | tf_op jit(solution)/shard_map/psum | solution.py:149
  (167 shorter events, 24.5 us)
Async XLA Ops:
  0.6 264.9 %copy-start = (bf16[128]{0:T(256)(128)(2,1)S(1)}, bf16[128]{0:T(256)(128)(2,1)}, u32[]{:S(2)}) copy-start(bf16[128]{0:T(256)(128)(2,1)} %param.30) | copy-start | bytes 772
  6.8 104.5 %all-to-all-start = ((bf16[4,32,1,9,3840]{4,1,3,2,0:T(8,128)(2,1)}), bf16[4,32,1,9,3840]{4,1,3,2,0:T(8,128)(2,1)}, u32[]{:S(2)}, u32[]{:S(2)}) async-start(bf16[4,32,1,9,3840]{4,1,3,2,0:T(8,128)(2,1)} %stack.2), calls=%async_computation | async-start | bytes 17694720 | tf_op jit(solution)/shard_map/all_to_all | solution.py:110
  132.7 29.5 %copy-start.6 = (f32[3,3,32]{2,1,0:T(4,128)S(1)}, f32[3,3,32]{2,1,0:T(4,128)}, u32[]{:S(2)}) copy-start(f32[3,3,32]{2,1,0:T(4,128)} %param.24) | copy-start | bytes 3460
  132.7 29.6 %copy-start.7 = (s32[2]{0:T(128)S(1)}, s32[2]{0:T(128)}, u32[]{:S(2)}) copy-start(s32[2]{0:T(128)} %param.22) | copy-start | bytes 28
  132.7 34.6 %copy-start.5 = (f32[32]{0:T(128)S(1)}, f32[32]{0:T(128)}, u32[]{:S(2)}) copy-start(f32[32]{0:T(128)} %param.25) | copy-start | bytes 388
  151.6 2.6 collective-permute-start
  152.9 3.1 %collective-permute-start.1 = (f32[1,128]{1,0:T(1,128)S(1)}, f32[1,128]{1,0:T(1,128)S(1)}, u32[]{:S(2)}, u32[]{:S(2)}) collective-permute-start(f32[1,128]{1,0:T(1,128)S(1)} %get-tuple-element.226), channel_id=1, source_target_pairs={{4,0},{8,4},{12,8},{5,1},{9,5},{13,9},{6,2},{10,6},{14,10},{7,3},{... | collective-permute-start | bytes 1544 | tf_op jit(solution)/shard_map/ppermute | solution.py:18
  156.1 6.8 %collective-permute-start.2 = (f32[130,1]{1,0:T(8,128)S(1)}, f32[130,1]{1,0:T(8,128)S(1)}, u32[]{:S(2)}, u32[]{:S(2)}) collective-permute-start(f32[130,1]{1,0:T(8,128)S(1)} %get-tuple-element.223), channel_id=1, source_target_pairs={{0,1},{1,2},{2,3},{4,5},{5,6},{6,7},{8,9},{9,10},{10,11},{12,13},{... | collective-permute-start | bytes 1568 | tf_op jit(solution)/shard_map/ppermute | solution.py:15
  160.9 6.2 %collective-permute-start.3 = (f32[130,1]{1,0:T(8,128)S(1)}, f32[130,1]{1,0:T(8,128)S(1)}, u32[]{:S(2)}, u32[]{:S(2)}) collective-permute-start(f32[130,1]{1,0:T(8,128)S(1)} %get-tuple-element.224), channel_id=1, source_target_pairs={{1,0},{2,1},{3,2},{5,4},{6,5},{7,6},{9,8},{10,9},{11,10},{13,12},{... | collective-permute-start | bytes 1568 | tf_op jit(solution)/shard_map/ppermute | solution.py:18
  167.3 36.2 %copy-start.1 = (bf16[3,3,64,32]{2,3,1,0:T(8,128)(2,1)S(1)}, bf16[3,3,64,32]{2,3,1,0:T(8,128)(2,1)}, u32[]{:S(2)}) copy-start(bf16[3,3,64,32]{2,3,1,0:T(8,128)(2,1)} %param.26) | copy-start | bytes 110596
  190.5 18.6 %copy-start.3 = (f32[64]{0:T(128)S(1)}, f32[64]{0:T(128)}, u32[]{:S(2)}) copy-start(f32[64]{0:T(128)} %param.27) | copy-start | bytes 772
  190.5 4.1 %collective-permute-start.4 = (bf16[32,1,64]{2,1,0:T(2,128)(2,1)S(1)}, bf16[32,1,64]{2,1,0:T(2,128)(2,1)S(1)}, u32[]{:S(2)}, u32[]{:S(2)}) collective-permute-start(bf16[32,1,64]{2,1,0:T(2,128)(2,1)S(1)} %get-tuple-element.217), channel_id=1, source_target_pairs={{0,4},{4,8},{8,12},{1,5},{5,9},{9,13},{2,6},{6,10},{10,14},{3,7},{... | collective-permute-start | bytes 12296 | tf_op jit(solution)/shard_map/ppermute | solution.py:15
  193.3 4.1 %collective-permute-start.5 = (bf16[32,1,64]{2,1,0:T(2,128)(2,1)S(1)}, bf16[32,1,64]{2,1,0:T(2,128)(2,1)S(1)}, u32[]{:S(2)}, u32[]{:S(2)}) collective-permute-start(bf16[32,1,64]{2,1,0:T(2,128)(2,1)S(1)} %get-tuple-element.218), channel_id=1, source_target_pairs={{4,0},{8,4},{12,8},{5,1},{9,5},{13,9},{6,2},{10,6},{14,10},{7,3},{... | collective-permute-start | bytes 12296 | tf_op jit(solution)/shard_map/ppermute | solution.py:18
  198.2 5.5 %collective-permute-start.6 = (bf16[32,66,1]{1,0,2:T(8,128)(2,1)S(1)}, bf16[32,66,1]{1,0,2:T(8,128)(2,1)S(1)}, u32[]{:S(2)}, u32[]{:S(2)}) collective-permute-start(bf16[32,66,1]{1,0,2:T(8,128)(2,1)S(1)} %copy.62), channel_id=1, source_target_pairs={{0,1},{1,2},{2,3},{4,5},{5,6},{6,7},{8,9},{9,10},{10,11},{12,13},{... | collective-permute-start | bytes 12680 | tf_op jit(solution)/shard_map/ppermute | solution.py:15
  202.0 5.5 %collective-permute-start.7 = (bf16[32,66,1]{1,0,2:T(8,128)(2,1)S(1)}, bf16[32,66,1]{1,0,2:T(8,128)(2,1)S(1)}, u32[]{:S(2)}, u32[]{:S(2)}) collective-permute-start(bf16[32,66,1]{1,0,2:T(8,128)(2,1)S(1)} %copy.63), channel_id=1, source_target_pairs={{1,0},{2,1},{3,2},{5,4},{6,5},{7,6},{9,8},{10,9},{11,10},{13,12},{... | collective-permute-start | bytes 12680 | tf_op jit(solution)/shard_map/ppermute | solution.py:18
  209.0 51.2 %copy-start.4 = (f32[128]{0:T(128)S(1)}, f32[128]{0:T(128)}, u32[]{:S(2)}) copy-start(f32[128]{0:T(128)} %param.29) | copy-start | bytes 1540
  242.1 5.0 %collective-permute-start.8 = (bf16[64,1,32]{0,2,1:T(8,128)(2,1)S(1)}, bf16[64,1,32]{0,2,1:T(8,128)(2,1)S(1)}, u32[]{:S(2)}, u32[]{:S(2)}) collective-permute-start(bf16[64,1,32]{0,2,1:T(8,128)(2,1)S(1)} %get-tuple-element.221), channel_id=1, source_target_pairs={{0,4},{4,8},{8,12},{1,5},{5,9},{9,13},{2,6},{6,10},{10,14},{3,7},{... | collective-permute-start | bytes 12296 | tf_op jit(solution)/shard_map/ppermute | solution.py:15
  245.1 4.0 %collective-permute-start.9 = (bf16[64,1,32]{0,2,1:T(8,128)(2,1)S(1)}, bf16[64,1,32]{0,2,1:T(8,128)(2,1)S(1)}, u32[]{:S(2)}, u32[]{:S(2)}) collective-permute-start(bf16[64,1,32]{0,2,1:T(8,128)(2,1)S(1)} %get-tuple-element.222), channel_id=1, source_target_pairs={{4,0},{8,4},{12,8},{5,1},{9,5},{13,9},{6,2},{10,6},{14,10},{7,3},{... | collective-permute-start | bytes 12296 | tf_op jit(solution)/shard_map/ppermute | solution.py:18
  250.0 6.5 %collective-permute-start.10 = (bf16[64,34,1]{0,2,1:T(2,128)(2,1)S(1)}, bf16[64,34,1]{0,2,1:T(2,128)(2,1)S(1)}, u32[]{:S(2)}, u32[]{:S(2)}) collective-permute-start(bf16[64,34,1]{0,2,1:T(2,128)(2,1)S(1)} %get-tuple-element.219), channel_id=1, source_target_pairs={{0,1},{1,2},{2,3},{4,5},{5,6},{6,7},{8,9},{9,10},{10,11},{12,13},{... | collective-permute-start | bytes 13064 | tf_op jit(solution)/shard_map/ppermute | solution.py:15
  253.5 5.6 %collective-permute-start.11 = (bf16[64,34,1]{0,2,1:T(2,128)(2,1)S(1)}, bf16[64,34,1]{0,2,1:T(2,128)(2,1)S(1)}, u32[]{:S(2)}, u32[]{:S(2)}) collective-permute-start(bf16[64,34,1]{0,2,1:T(2,128)(2,1)S(1)} %get-tuple-element.220), channel_id=1, source_target_pairs={{1,0},{2,1},{3,2},{5,4},{6,5},{7,6},{9,8},{10,9},{11,10},{13,12},{... | collective-permute-start | bytes 13064 | tf_op jit(solution)/shard_map/ppermute | solution.py:18
  266.0 15.1 %copy-start.2 = (f32[32,32]{1,0:T(8,128)}, f32[32,32]{1,0:T(8,128)S(1)}, u32[]{:S(2)}) copy-start(f32[32,32]{1,0:T(8,128)S(1)} %broadcast_add_fusion) | copy-start | bytes 12292
